TPU v7x, 512 devices: a whole 4x8x8 slice. The times are simulated.
512 devices in a mesh: pair: 64 (over x, z, core), win: 8 (over y).
Axes of the slice: x: 4, y: 8, z: 8, core: 2. Of those that a mesh axis runs over, the one named last changes fastest.
Arguments:
- windows: bfloat16 [8, 2048, 8192], P('win', None, 'pair'), may hold values from -4 to 4
- pair_offset: int32 [64, 4], P('pair'), may hold values from 1 to 4, as said below
- pair_count: int32 [64], P('pair'), may hold values from 0 to 4, as said below
- pair_mask: int32 [256, 128], P('pair'), may hold values 0 or 1
Outputs:
- stacks: float32 [512, 256, 128], P('win', 'pair')
Inputs may be any that keep to these rules, and one draw needn't show every extreme that they name: Row d holds the numbers 1 to 4, each once; slots from pair_count[d] on are empty; every live slot's partner block d + pair_offset[d, s] is below 64; for d >= 60 the row is 1, 2, ... in order. `pair_count`: block d >= 60 owns 64 - 1 - d live pair blocks; block 59 owns 4.
All inputs are finite; a program needn't handle non-finite values. No bound on the sum of `pair_mask` on one device may be relied on, other than what follows from the above.
Results may differ from a plain program's by a relative error of at most 0.01.
Values may be sent and summed in bfloat16 or wider, within the bound.
A program may use at most 64 MiB of HBM per device.

v0:
```python
import math

import jax
import jax.numpy as jnp
from jax import lax
from jax.sharding import PartitionSpec as P

FB = 512
F0 = 64
LAGS = 512


def shifted(block, axis, distance):
    devices = range(lax.axis_size(axis))
    route = [(i - distance, i) for i in devices if i - distance in devices]
    return lax.ppermute(block, axis, route)


def band_table(band_first, band_width, length):
    nfft = 2 * length
    frequency = F0 + band_first + jnp.arange(band_width, dtype=jnp.int32)
    samples = jnp.arange(length, dtype=jnp.int32)
    phases = (frequency[:, None] * samples[None, :] % nfft).astype(jnp.float32) * (
        2.0 * math.pi / nfft
    )
    return jnp.concatenate([jnp.cos(phases), -jnp.sin(phases)], axis=0)


def spectrum(frames):
    length = frames.shape[1]
    band_block = min(FB, 128)
    band_parts = FB // band_block

    def one_part(part_index):
        dft_table = band_table(part_index * band_block, band_block, length)
        table_high = dft_table.astype(jnp.bfloat16)
        table_rest = (dft_table - table_high.astype(jnp.float32)).astype(jnp.bfloat16)
        upper = jnp.einsum("kn,wnc->wkc", table_high, frames, preferred_element_type=jnp.float32)
        lower = jnp.einsum("kn,wnc->wkc", table_rest, frames, preferred_element_type=jnp.float32)
        return (upper + lower).astype(jnp.bfloat16)

    return lax.map(one_part, jnp.arange(band_parts, dtype=jnp.int32))


def correlate(own_spectra, other_spectra, mask_row):
    half_rows = own_spectra.shape[2] // 2
    own_wide = own_spectra.astype(jnp.float32)
    other_wide = other_spectra.astype(jnp.float32)
    own_real = own_wide[:, :, :half_rows]
    own_imag = own_wide[:, :, half_rows:]
    other_real = other_wide[:, :, :half_rows]
    other_imag = other_wide[:, :, half_rows:]
    real_sum = jnp.sum(own_real * other_real + own_imag * other_imag, axis=1)
    imag_sum = jnp.sum(own_imag * other_real - own_real * other_imag, axis=1)
    weight = mask_row.astype(jnp.float32)
    return jnp.stack([real_sum, imag_sum], axis=1) * weight


def inverse_rows(row_count, length, factor):
    nfft = 2 * length
    band_block = min(FB, 128)
    band_parts = FB // band_block
    lag_values = jnp.arange(row_count, dtype=jnp.int32) - LAGS // 2
    frequency = F0 + jnp.arange(FB, dtype=jnp.int32).reshape(band_parts, band_block)
    phases = (lag_values[:, None, None] * frequency[None] % nfft).astype(jnp.float32) * (
        2.0 * math.pi / nfft
    )
    return (jnp.stack([jnp.cos(phases), -jnp.sin(phases)], axis=2) * factor).reshape(
        row_count, 2 * FB
    )


def local(windows, pair_offset, pair_count, pair_mask):
    length = windows.shape[1]
    own_spectra = spectrum(windows)
    slot_offsets = pair_offset[0]
    live_count = pair_count[0]
    reach_total = slot_offsets.shape[0]
    neighbours = jnp.stack(
        [shifted(windows, "pair", -offset_step) for offset_step in range(1, reach_total + 1)]
    )

    def visit_slot(position, buffer):
        chosen = lax.dynamic_index_in_dim(slot_offsets, position, 0, keepdims=False) - 1
        other_block = lax.dynamic_index_in_dim(neighbours, chosen, 0, keepdims=False)
        mask_row = lax.dynamic_index_in_dim(pair_mask, position, 0, keepdims=False)
        return lax.dynamic_update_index_in_dim(
            buffer, correlate(own_spectra, spectrum(other_block), mask_row), position, 0
        )

    zero_cross = jnp.zeros(
        (reach_total, own_spectra.shape[0], 2, own_spectra.shape[2] // 2, own_spectra.shape[3]),
        jnp.float32,
    )
    cross_sum = lax.fori_loop(0, live_count, visit_slot, zero_cross)
    flat_cross = cross_sum.reshape(reach_total, 2 * FB, cross_sum.shape[-1])
    windows_total = windows.shape[0] * lax.axis_size("win")
    factor = 1.0 / (length * math.sqrt(FB * windows_total))
    lag_share = LAGS // lax.axis_size("win")
    return lax.psum_scatter(
        jnp.einsum(
            "lk,skc->lsc",
            inverse_rows(lag_share * lax.axis_size("win"), length, factor),
            flat_cross,
            precision=lax.Precision.HIGHEST,
        ),
        "win",
        scatter_dimension=0,
        tiled=True,
    )


def solution(mesh):
    placed = (P("win", None, "pair"), P("pair", None), P("pair"), P("pair", None))
    return jax.shard_map(
        local, mesh=mesh, in_specs=placed, out_specs=P("win", "pair", None), check_vma=False
    )
```

profile of v0, /device:TPU:1, one launch (start us, length us, event | category | flops | bytes accessed | tf_op | source)
XLA Modules:
  0.0 244.6 jit_solution(1059960014872012967)
XLA Ops:
  6.5 0.0 reduce-scatter.2.cloned.1.call-start
  6.5 1.3 collective-permute-start.3
  7.8 1.3 collective-permute-start.2
  9.1 1.3 collective-permute-start.1
  10.4 8.8 %collective-permute-start = (bf16[1,2048,128]{2,1,0:T(8,128)(2,1)}, bf16[1,2048,128]{2,1,0:T(8,128)(2,1)}, u32[]{:S(2)}, u32[]{:S(2)}) collective-permute-start(bf16[1,2048,128]{2,1,0:T(8,128)(2,1)} %param.10), channel_id=1, source_target_pairs={{8,0},{16,8},{24,16},{32,24},{40,32},{48,40},{56,48},{64,56},{72,6... | collective-permute-start | bytes 1572872 | tf_op jit(solution)/shard_map/ppermute | solution.py:16
  19.2 25.0 %while.51 = (s32[]{:T(128)}, bf16[4,1,256,128]{3,2,1,0:T(8,128)(2,1)S(1)}, s32[4]{0:T(128)S(1)}, bf16[1,2048,128]{2,1,0:T(8,128)(2,1)}, s32[]{:T(128)}, /*index=5*/s32[1]{0:T(128)}, s32[1]{0:T(128)}) while((s32[]{:T(128)}, bf16[4,1,256,128]{3,2,1,0:T(8,128)(2,1)S(1)}, s32[4]{0:T(128)S(1)}, bf16[1,2048,128]{2,1,0:T(8,128)(2,1)}, s32[]{:T(128)}, ...), condition=%wide.region_1.2_spmd, body=%wide.region_0.1_spmd.sunk | while | flops 277151872 | bytes 9766045 | solution.py:42
  19.3 0.0 copy-start
  19.3 0.6 dynamic_slice.54
  20.4 4.2 %fusion.88 = (f32[128,2048]{1,0:T(8,128)S(1)}, f32[128,2048]{1,0:T(8,128)S(1)}) fusion(s32[128]{0:T(128)S(1)} %iota_add_fusion.5), kind=kLoop, calls=%fused_computation.21.clone.1 | loop fusion | flops 3932160 | bytes 2097664 | tf_op jit(solution)/shard_map/while/body/eval_jaxpr/cos | solution.py:26
  24.6 0.0 copy-done
  24.6 0.4 fusion.89
  25.0 0.5 fusion.90
  25.5 0.0 copy-start
  25.5 0.6 dynamic_slice.54
  26.7 4.2 %fusion.88 = (f32[128,2048]{1,0:T(8,128)S(1)}, f32[128,2048]{1,0:T(8,128)S(1)}) fusion(s32[128]{0:T(128)S(1)} %iota_add_fusion.5), kind=kLoop, calls=%fused_computation.21.clone.1 | loop fusion | flops 3932160 | bytes 2097664 | tf_op jit(solution)/shard_map/while/body/eval_jaxpr/cos | solution.py:26
  30.9 0.0 copy-done
  30.9 0.4 fusion.89
  31.3 0.5 fusion.90
  31.8 0.0 copy-start
  31.8 0.6 dynamic_slice.54
  32.9 4.2 %fusion.88 = (f32[128,2048]{1,0:T(8,128)S(1)}, f32[128,2048]{1,0:T(8,128)S(1)}) fusion(s32[128]{0:T(128)S(1)} %iota_add_fusion.5), kind=kLoop, calls=%fused_computation.21.clone.1 | loop fusion | flops 3932160 | bytes 2097664 | tf_op jit(solution)/shard_map/while/body/eval_jaxpr/cos | solution.py:26
  37.1 0.0 copy-done
  37.1 0.4 fusion.89
  37.5 0.5 fusion.90
  38.0 0.0 copy-start
  38.0 0.6 dynamic_slice.54
  39.2 4.2 %fusion.88 = (f32[128,2048]{1,0:T(8,128)S(1)}, f32[128,2048]{1,0:T(8,128)S(1)}) fusion(s32[128]{0:T(128)S(1)} %iota_add_fusion.5), kind=kLoop, calls=%fused_computation.21.clone.1 | loop fusion | flops 3932160 | bytes 2097664 | tf_op jit(solution)/shard_map/while/body/eval_jaxpr/cos | solution.py:26
  43.4 0.0 copy-done
  43.4 0.4 fusion.89
  43.8 0.5 fusion.90
  44.3 5.8 %fusion.68 = (f32[512,4,1,128]{3,0,2,1:T(8,128)}, f32[512,4,1,128]{3,0,2,1:T(8,128)}) fusion(s32[4,128]{1,0:T(4,128)S(1)} %add_add_fusion, s32[512]{0:T(512)S(1)} %iota_add_fusion.2), kind=kLoop, calls=%fused_computation.76 | loop fusion | flops 3932160 | bytes 2101248 | tf_op jit(solution)/shard_map/cos | solution.py:68
  50.1 0.0 collective-permute-done.3
  50.1 5.5 %collective-permute-done.2 = bf16[1,2048,128]{2,1,0:T(8,128)(2,1)S(1)} collective-permute-done((bf16[1,2048,128]{2,1,0:T(8,128)(2,1)}, bf16[1,2048,128]{2,1,0:T(8,128)(2,1)S(1)}, u32[]{:S(2)}, u32[]{:S(2)}) %collective-permute-start.2) | collective-permute-done | bytes 524320 | tf_op jit(solution)/shard_map/ppermute | solution.py:16
  55.6 0.1 collective-permute-done.1
  55.7 0.9 collective-permute-done
  56.6 1.5 pad_maximum_fusion.2
  58.1 0.0 copy-start.1
  58.1 1.6 broadcast_in_dim.25.clone
  59.7 29.8 %while.53 = (s32[]{:T(128)}, f32[4,4,2,128,128]{4,3,2,0,1:T(8,128)}, s32[]{:T(128)}, bf16[4,1,256,128]{3,2,0,1:T(8,128)(2,1)S(1)}, s32[4]{0:T(128)S(1)}, /*index...) while((s32[]{:T(128)}, ...), condition=%wide.region_5.6_spmd, body=%wide.region_2.5_spmd.sunk | while | flops 278069504 | bytes 12913614 | solution.py:95
  60.5 0.6 dynamic_slice.57
  62.3 24.8 %while.54 = (s32[]{:T(128)}, bf16[4,1,256,128]{3,2,1,0:T(8,128)(2,1)S(1)}, s32[4]{0:T(128)S(1)}, bf16[1,2048,128]{2,1,0:T(8,128)(2,1)S(1)}, s32[]{:T(128)}, /*index=5*/s32[1]{0:T(128)}, s32[1]{0:T(128)}) while((s32[]{:T(128)}, bf16[4,1,256,128]{3,2,1,0:T(8,128)(2,1)S(1)}, s32[4]{0:T(128)S(1)}, bf16[1,2048,128]{2,1,0:T(8,128)(2,1)S(1)}, ...), condition=%wide.region_4.4_spmd, body=%wide.region_3.3_spmd.sunk | while | flops 277151872 | bytes 7668865 | solution.py:42
  62.4 0.6 dynamic_slice.58
  63.5 4.2 %fusion.95 = (f32[128,2048]{1,0:T(8,128)S(1)}, f32[128,2048]{1,0:T(8,128)S(1)}) fusion(s32[128]{0:T(128)S(1)} %iota_add_fusion.6), kind=kLoop, calls=%fused_computation.46.clone.1 | loop fusion | flops 3932160 | bytes 2097664 | tf_op jit(solution)/shard_map/while/body/while/body/eval_jaxpr/cos | solution.py:26
  67.7 0.4 fusion.96
  68.1 0.5 fusion.97
  68.6 0.6 dynamic_slice.58
  69.7 4.2 %fusion.95 = (f32[128,2048]{1,0:T(8,128)S(1)}, f32[128,2048]{1,0:T(8,128)S(1)}) fusion(s32[128]{0:T(128)S(1)} %iota_add_fusion.6), kind=kLoop, calls=%fused_computation.46.clone.1 | loop fusion | flops 3932160 | bytes 2097664 | tf_op jit(solution)/shard_map/while/body/while/body/eval_jaxpr/cos | solution.py:26
  73.8 0.4 fusion.96
  74.3 0.5 fusion.97
  74.7 0.6 dynamic_slice.58
  75.9 4.2 %fusion.95 = (f32[128,2048]{1,0:T(8,128)S(1)}, f32[128,2048]{1,0:T(8,128)S(1)}) fusion(s32[128]{0:T(128)S(1)} %iota_add_fusion.6), kind=kLoop, calls=%fused_computation.46.clone.1 | loop fusion | flops 3932160 | bytes 2097664 | tf_op jit(solution)/shard_map/while/body/while/body/eval_jaxpr/cos | solution.py:26
  80.0 0.4 fusion.96
  80.5 0.5 fusion.97
  80.9 0.6 dynamic_slice.58
  82.1 4.2 %fusion.95 = (f32[128,2048]{1,0:T(8,128)S(1)}, f32[128,2048]{1,0:T(8,128)S(1)}) fusion(s32[128]{0:T(128)S(1)} %iota_add_fusion.6), kind=kLoop, calls=%fused_computation.46.clone.1 | loop fusion | flops 3932160 | bytes 2097664 | tf_op jit(solution)/shard_map/while/body/while/body/eval_jaxpr/cos | solution.py:26
  86.2 0.4 fusion.96
  86.7 0.5 fusion.97
  87.2 0.1 add_bitcast_fusion.2
  87.3 0.7 fusion.91
  88.0 0.8 copy_dynamic-update-slice_fusion.2
  89.5 6.7 %fusion.61 = f32[512,4,128]{2,0,1:T(8,128)} fusion(f32[4,4,2,128,128]{4,3,2,0,1:T(8,128)} %get-tuple-element.276, f32[512,4,1,128]{3,0,2,1:T(8,128)} %get-tuple-element.321, f32[512,4,1,128]{3,0,2,1:T(8,128)} %get-tuple-element.320), kind=kOutput, calls=%fused_computation.70 | convolution fusion | flops 3222274048 | bytes 5242880 | tf_op jit(solution)/shard_map/lk,skc->lsc/dot_general | solution.py:101
  96.2 0.0 reduce-scatter.2.cloned.1.call-update
  96.2 139.9 %reduce-scatter.2.cloned.1.call-done = f32[64,4,128]{2,0,1:T(8,128)} async-done(((f32[512,4,128]{2,0,1:T(8,128)}), f32[64,4,128]{2,0,1:T(8,128)}) %reduce-scatter.2.cloned.1.call-update) | async-done | bytes 131088 | tf_op jit(solution)/shard_map/reduce_scatter | solution.py:100
  236.1 1.6 copy.8
  (18 shorter events, 0.2 us)
Async XLA Ops:
  6.5 229.5 %reduce-scatter.2.cloned.1.call-start = ((), (), s32[]{:S(2)}) async-start(), calls=%async_computation.1 | async-start | bytes 1179648 | tf_op jit(solution)/shard_map/reduce_scatter | solution.py:100
  6.5 43.6 %collective-permute-start.3 = (bf16[1,2048,128]{2,1,0:T(8,128)(2,1)}, bf16[1,2048,128]{2,1,0:T(8,128)(2,1)S(1)}, u32[]{:S(2)}, u32[]{:S(2)}) collective-permute-start(bf16[1,2048,128]{2,1,0:T(8,128)(2,1)} %param.10), channel_id=1, source_target_pairs={{32,0},{40,8},{48,16},{56,24},{64,32},{72,40},{80,48},{88,56},{96,... | collective-permute-start | bytes 1572872 | tf_op jit(solution)/shard_map/ppermute | solution.py:16
  7.8 47.8 %collective-permute-start.2 = (bf16[1,2048,128]{2,1,0:T(8,128)(2,1)}, bf16[1,2048,128]{2,1,0:T(8,128)(2,1)S(1)}, u32[]{:S(2)}, u32[]{:S(2)}) collective-permute-start(bf16[1,2048,128]{2,1,0:T(8,128)(2,1)} %param.10), channel_id=1, source_target_pairs={{24,0},{32,8},{40,16},{48,24},{56,32},{64,40},{72,48},{80,56},{88,... | collective-permute-start | bytes 1572872 | tf_op jit(solution)/shard_map/ppermute | solution.py:16
  9.1 46.6 %collective-permute-start.1 = (bf16[1,2048,128]{2,1,0:T(8,128)(2,1)}, bf16[1,2048,128]{2,1,0:T(8,128)(2,1)}, u32[]{:S(2)}, u32[]{:S(2)}) collective-permute-start(bf16[1,2048,128]{2,1,0:T(8,128)(2,1)} %param.10), channel_id=1, source_target_pairs={{16,0},{24,8},{32,16},{40,24},{48,32},{56,40},{64,48},{72,56},{80,... | collective-permute-start | bytes 1572872 | tf_op jit(solution)/shard_map/ppermute | solution.py:16
  10.4 46.2 %collective-permute-start = (bf16[1,2048,128]{2,1,0:T(8,128)(2,1)}, bf16[1,2048,128]{2,1,0:T(8,128)(2,1)}, u32[]{:S(2)}, u32[]{:S(2)}) collective-permute-start(bf16[1,2048,128]{2,1,0:T(8,128)(2,1)} %param.10), channel_id=1, source_target_pairs={{8,0},{16,8},{24,16},{32,24},{40,32},{48,40},{56,48},{64,56},{72,6... | collective-permute-start | bytes 1572872 | tf_op jit(solution)/shard_map/ppermute | solution.py:16
  19.3 5.3 %copy-start = (bf16[1,2048,128]{2,1,0:T(8,128)(2,1)S(1)}, bf16[1,2048,128]{2,1,0:T(8,128)(2,1)}, u32[]{:S(2)}) copy-start(bf16[1,2048,128]{2,1,0:T(8,128)(2,1)} %get-tuple-element.477) | copy-start | bytes 1572868 | tf_op jit(solution)/shard_map/while
  25.5 5.3 %copy-start = (bf16[1,2048,128]{2,1,0:T(8,128)(2,1)S(1)}, bf16[1,2048,128]{2,1,0:T(8,128)(2,1)}, u32[]{:S(2)}) copy-start(bf16[1,2048,128]{2,1,0:T(8,128)(2,1)} %get-tuple-element.477) | copy-start | bytes 1572868 | tf_op jit(solution)/shard_map/while
  31.8 5.3 %copy-start = (bf16[1,2048,128]{2,1,0:T(8,128)(2,1)S(1)}, bf16[1,2048,128]{2,1,0:T(8,128)(2,1)}, u32[]{:S(2)}) copy-start(bf16[1,2048,128]{2,1,0:T(8,128)(2,1)} %get-tuple-element.477) | copy-start | bytes 1572868 | tf_op jit(solution)/shard_map/while
  38.0 5.3 %copy-start = (bf16[1,2048,128]{2,1,0:T(8,128)(2,1)S(1)}, bf16[1,2048,128]{2,1,0:T(8,128)(2,1)}, u32[]{:S(2)}) copy-start(bf16[1,2048,128]{2,1,0:T(8,128)(2,1)} %get-tuple-element.477) | copy-start | bytes 1572868 | tf_op jit(solution)/shard_map/while
  58.1 1.6 copy-start.1
Sparse Core Ops, SparseCore 0:
  96.3 139.7 reduce-scatter.1
where the time goes:
time: 249 us; the launch traced here: 245 us
  waiting for transfers between devices  146 us (59%)
  other arithmetic  42.3 us (17%)
  matrix products  13.8 us (6%)
  between operations  13.5 us (5%)
  starting transfers between devices  12.7 us (5%)
  local copies, waits for them, and re-layouts  8.43 us (3%)
  loops' own time  7.56 us (3%)
    reduce_scatter x1, waiting for transfers between devices, local(): lax.psum_scatter(jnp.einsum('lk,skc->lsc', inverse_rows(lag_share * lax.a...  140 us
    cos x8, other arithmetic, band_table(): return jnp.concatenate([jnp.cos(phases), -jnp.sin(phases)], axis=0)  33.3 us
    ppermute x4, starting transfers between devices, shifted(): return lax.ppermute(block, axis, route)  12.7 us
    dot_general x1, matrix products, local(): jnp.einsum('lk,skc->lsc', inverse_rows(lag_share * lax.axis_size('win'),...  6.72 us
    ppermute x4, waiting for transfers between devices, shifted(): return lax.ppermute(block, axis, route)  6.49 us
    cos x1, other arithmetic, inverse_rows(): jnp.cos(phases)  5.84 us
  transfers between devices with their start and end apart: 5, of which 4 were waited for; matrix products, arithmetic and copies ran while one was open for 12% of the time, Pallas kernels for 0%

commit v1 on v0

v1 whole, which is shorter than its diff:
```python
import functools
import math

import jax
import jax.numpy as jnp
import numpy as np
from jax import lax
from jax.experimental import pallas as pl
from jax.experimental.pallas import tpu as pltpu
from jax.sharding import PartitionSpec as P

FB = 512
F0 = 64
LAGS = 512
LENGTH = 2048
CH = 128
SPLIT = 4
FOLD = LENGTH // SPLIT
QUARTERS = 4
HALVES = 2
ROWS = 8
SEND = jnp.bfloat16
MESH = pl.DeviceIdType.MESH
PAIRS = ((2, 3), (2, 4), (2, 5), (3, 4), (3, 5), (0, 4), (1, 4), (1, 5))
TILES = ((0, 1), (2, 2), (3, 4), (5, 5), (6, 7))


def quarter_bins(quarter):
    steps = 8 * np.arange(FB // 8)
    return np.concatenate([steps + 2 * quarter, steps + 2 * quarter + 1])


def two_parts(table):
    high = table.astype(jnp.bfloat16)
    rest = (table - high.astype(np.float64)).astype(jnp.bfloat16)
    return high, rest


def forward_table():
    nfft = 2 * LENGTH
    parts = []
    for quarter in range(QUARTERS):
        phase = 2 * np.pi * ((F0 + quarter_bins(quarter))[:, None] * np.arange(FOLD)[None, :] % nfft) / nfft
        table = np.concatenate([np.cos(phase), -np.sin(phase)], axis=0)
        parts.append(np.concatenate(two_parts(table), axis=1))
    return np.stack(parts)


def lag_turns():
    bins = np.concatenate([quarter_bins(quarter) for quarter in range(QUARTERS)])
    phase = 2 * np.pi * ((F0 + bins) * (LAGS // 2) % (2 * LENGTH)) / (2 * LENGTH)
    return np.stack([np.cos(phase), np.sin(phase)]).astype(np.float32)


def weighted(terms):
    total = None
    for weight, value in terms:
        if abs(weight) < 1e-9:
            continue
        if abs(abs(weight) - 1.0) > 1e-9:
            value = value * np.float32(abs(weight))
        if total is None:
            total = value if weight > 0 else -value
        else:
            total = total + value if weight > 0 else total - value
    return total


def kernel(
    chips, wins, factor, x_hbm, fwd_hbm, turn_ref, off_ref, cnt_ref, mask_ref, out_ref,
    xbuf, fwd, spec, gath, acc, res, fin,
    load_sem, a_send, a_recv, z_send, z_recv, f_send, f_recv,
):
    pair, win = lax.axis_index("pair"), lax.axis_index("win")
    chip, core = pair // 2, pair % 2
    before, after = (chip + chips - 1) % chips, (chip + 1) % chips
    group = win * 2 + core
    groups = 2 * wins

    x_copy = pltpu.make_async_copy(x_hbm.at[0], xbuf, load_sem.at[0])
    x_copy.start()
    fwd_copies = []
    for quarter in range(QUARTERS):
        copy = pltpu.make_async_copy(fwd_hbm.at[quarter], fwd.at[quarter], load_sem.at[1 + quarter])
        copy.start()
        fwd_copies.append(copy)

    barrier = pltpu.get_barrier_semaphore()

    def greet(step, carry):
        there, side = (win + step // 2) % wins, (core + step % 2) % 2

        @pl.when(step > 0)
        def _():
            pl.semaphore_signal(barrier, inc=1, device_id=(2 * chip + side, there), device_id_type=MESH)

        pl.semaphore_signal(barrier, inc=1, device_id=(2 * after + side, there), device_id_type=MESH)
        return carry

    lax.fori_loop(0, groups, greet, 0)
    pl.semaphore_signal(barrier, inc=1, device_id=(2 * before + core, win), device_id_type=MESH)

    acc[...] = jnp.zeros_like(acc)

    def near(step):
        turn = (step % 2) * ((step + 1) // 2) + (1 - step % 2) * (wins - step // 2)
        return (win + turn) % wins

    def exchange(half, there, side):
        return pltpu.make_async_remote_copy(
            src_ref=spec.at[half, there * 2 + side],
            dst_ref=gath.at[1, win, core, half],
            send_sem=a_send.at[half, there, side],
            recv_sem=a_recv.at[half, win, core],
            device_id=(2 * chip + side, there),
            device_id_type=MESH,
        )

    def arrival(half, there, side):
        return pltpu.make_async_remote_copy(
            src_ref=spec.at[half, there * 2 + side],
            dst_ref=gath.at[1, there, side, half],
            send_sem=a_send.at[half, there, side],
            recv_sem=a_recv.at[half, there, side],
            device_id=(2 * chip + side, there),
            device_id_type=MESH,
        )

    x_copy.wait()
    for half in range(HALVES):
        for part in range(QUARTERS // HALVES):
            quarter = half * (QUARTERS // HALVES) + part
            fwd_copies[quarter].wait()
            wide = jnp.concatenate([xbuf[h * FOLD:(h + 1) * FOLD, :] for h in range(SPLIT)], axis=1)
            whole = jnp.dot(fwd[quarter, :, :FOLD], wide, preferred_element_type=jnp.float32)
            whole += jnp.dot(fwd[quarter, :, FOLD:], wide, preferred_element_type=jnp.float32)
            reals, imags = [], []
            for odd in range(2):
                residue = 2 * quarter + odd
                real_terms, imag_terms = [], []
                for h in range(SPLIT):
                    turn = 2 * math.pi * ((residue * h) % 8) / 8
                    real = whole[odd * 64:odd * 64 + 64, h * CH:(h + 1) * CH]
                    imag = whole[128 + odd * 64:128 + odd * 64 + 64, h * CH:(h + 1) * CH]
                    real_terms += [(math.cos(turn), real), (math.sin(turn), imag)]
                    imag_terms += [(math.cos(turn), imag), (-math.sin(turn), real)]
                reals.append(weighted(real_terms))
                imags.append(weighted(imag_terms))
            for kind, value in enumerate((reals, imags)):
                turned = jnp.concatenate(value, axis=0).T.reshape(groups, ROWS, 128)
                lane = part * 256 + kind * 128
                spec[half, :, :, lane:lane + 128] = turned.astype(jnp.bfloat16)
        if half == 0:
            pl.semaphore_wait(barrier, 2 * groups)

        def send(step, carry, half=half):
            there, side = near(step // 2), (core + step % 2) % 2
            exchange(half, there, side).start()
            return carry

        lax.fori_loop(1, groups, send, 0)
        gath[1, win, core, half] = spec[half, group]

    def forward(there, up):
        return pltpu.make_async_remote_copy(
            src_ref=gath.at[1, there],
            dst_ref=gath.at[0 if up else 2, there],
            send_sem=z_send.at[1 if up else 0, there],
            recv_sem=z_recv.at[0 if up else 1, there],
            device_id=(2 * (after if up else before) + core, win),
            device_id_type=MESH,
        )

    def multiply(there):
        for quarter in range(QUARTERS):
            half, lane = quarter // (QUARTERS // HALVES), quarter % (QUARTERS // HALVES) * 256
            blocks = []
            for block in range(6):
                both = gath[block // 2, there, block % 2, half, :, lane:lane + 256].astype(jnp.float32)
                blocks.append((both[:, :128], both[:, 128:]))
            for index, (own, other) in enumerate(PAIRS):
                (own_real, own_imag), (other_real, other_imag) = blocks[own], blocks[other]
                rows = slice(index * ROWS, index * ROWS + ROWS)
                left = slice(quarter * 256, quarter * 256 + 128)
                right = slice(quarter * 256 + 128, quarter * 256 + 256)
                acc[rows, left] += own_real * other_real + own_imag * other_imag
                acc[rows, right] += own_imag * other_real - own_real * other_imag

    lag = 3

    def travel(step, carry):
        @pl.when(step < wins)
        def _():
            there = near(step)
            for half in range(HALVES):
                arrival(half, there, 1 - core).wait_recv()

                @pl.when(step > 0)
                def _():
                    arrival(half, there, core).wait_recv()
            forward(there, True).start()
            forward(there, False).start()

        @pl.when(step >= lag)
        def _():
            there = near(step - lag)
            forward(there, True).wait_recv()
            forward(there, False).wait_recv()
            multiply(there)
        return carry

    lax.fori_loop(0, wins + lag, travel, 0)

    count = len(PAIRS) * ROWS
    stacks = jnp.zeros((count, LAGS), jnp.float32)
    for quarter in range(QUARTERS):
        bins = slice(quarter * 128, quarter * 128 + 128)
        cosine, sine = turn_ref[0:1, bins] * factor, turn_ref[1:2, bins] * factor
        real = acc[:, quarter * 256:quarter * 256 + 128]
        imag = acc[:, quarter * 256 + 128:quarter * 256 + 256]
        cross = jnp.concatenate([real * cosine + imag * sine, imag * cosine - real * sine], axis=1)
        high = cross.astype(jnp.bfloat16)
        rest = (cross - high.astype(jnp.float32)).astype(jnp.bfloat16)
        both = jnp.concatenate([high, rest], axis=0)
        upper = jnp.dot(both, fwd[quarter, :, :FOLD], preferred_element_type=jnp.float32)
        stacks += upper[:count] + upper[count:]
        stacks += jnp.dot(high, fwd[quarter, :, FOLD:], preferred_element_type=jnp.float32)
    lanes = lax.broadcasted_iota(jnp.int32, (ROWS, 128), 1)
    for column in range(LAGS // 128):
        for tile, (left, right) in enumerate(TILES):
            a = stacks[left * ROWS:(left + 1) * ROWS, column * 128:(column + 1) * 128]
            b = stacks[right * ROWS:(right + 1) * ROWS, column * 128:(column + 1) * 128]
            even = jnp.where(lanes < 64, a, pltpu.roll(b, 64, 1))
            odd = jnp.where(lanes < 64, pltpu.roll(a, 64, 1), b)
            res[2 * column, tile] = even.astype(SEND)
            res[2 * column + 1, tile] = odd.astype(SEND)

    def deliver(there, kind):
        first, size, slot = ((0, 2, 0), (2, 1, 0), (3, 1, 2), (4, 1, 2))[kind]
        where = chip if kind < 2 else before
        return pltpu.make_async_remote_copy(
            src_ref=res.at[there, first:first + size],
            dst_ref=fin.at[group, slot:slot + size],
            send_sem=f_send.at[kind, there],
            recv_sem=f_recv.at[0 if kind < 2 else 1],
            device_id=(2 * where + kind % 2, there),
            device_id_type=MESH,
        )

    def hand_out(step, carry):
        there = (win + step) % wins
        for kind in (2, 3, 0, 1):
            if kind < 2:
                @pl.when((step > 0) | (core != kind))
                def _():
                    deliver(there, kind).start()
            else:
                deliver(there, kind).start()
        return carry

    lax.fori_loop(0, wins, hand_out, 0)

    @pl.when(core == 0)
    def _():
        fin[group, 0:2] = res[win, 0:2]
        others = fin.at[0:groups - 1, 0:2]
        pltpu.make_async_copy(others, others, f_recv.at[0]).wait()

    @pl.when(core == 1)
    def _():
        fin[group, 0:1] = res[win, 2:3]
        others = fin.at[0:groups - 1, 0:1]
        pltpu.make_async_copy(others, others, f_recv.at[0]).wait()

    everyone = fin.at[:, 2:3]
    pltpu.make_async_copy(everyone, everyone, f_recv.at[1]).wait()

    first = fin[:, 0].astype(jnp.float32).reshape(CH, 128)
    third = fin[:, 1].astype(jnp.float32).reshape(CH, 128)
    last = fin[:, 2].astype(jnp.float32).reshape(CH, 128)
    wide_lanes = lax.broadcasted_iota(jnp.int32, (CH, 128), 1)
    second = jnp.where((wide_lanes < 64) & (core == 0), third, last)
    first, second = first.T, second.T
    choices = (first[:64], first[64:], second[:64], second[64:])
    for slot in range(4):
        offset = off_ref[0, slot]
        picked = choices[3]
        for index in range(3):
            picked = jnp.where(offset == index + 1, choices[index], picked)
        weight = mask_ref[slot:slot + 1, :].astype(jnp.float32)
        picked = jnp.where(slot < cnt_ref[0, 0], picked * weight, 0.0)
        out_ref[pl.ds(slot, 64, stride=4), :] = picked

    def finish(step, carry):
        there, side = step // 2, step % 2

        @pl.when(step != group)
        def _():
            for half in range(HALVES):
                exchange(half, there, side).wait_send()
        return carry

    lax.fori_loop(0, groups, finish, 0)

    def finish_rest(step, carry):
        forward(step, True).wait_send()
        forward(step, False).wait_send()
        for kind in range(4):
            if kind < 2:
                @pl.when((step != win) | (core != kind))
                def _():
                    deliver(step, kind).wait_send()
            else:
                deliver(step, kind).wait_send()
        return carry

    lax.fori_loop(0, wins, finish_rest, 0)


def local(chips, wins, windows, pair_offset, pair_count, pair_mask):
    groups = 2 * wins
    fwd_table = jnp.asarray(forward_table())
    factor = 1.0 / (LENGTH * math.sqrt(FB * windows.shape[0] * wins))
    hbm = pl.BlockSpec(memory_space=pltpu.HBM)
    smem = pl.BlockSpec(memory_space=pltpu.SMEM)
    vmem = pl.BlockSpec(memory_space=pltpu.VMEM)
    out = pl.pallas_call(
        functools.partial(kernel, chips, wins, factor),
        out_shape=jax.ShapeDtypeStruct((LAGS // wins * 4, CH), jnp.float32),
        in_specs=[hbm, hbm, vmem, smem, smem, vmem],
        out_specs=vmem,
        scratch_shapes=[
            pltpu.VMEM((LENGTH, CH), jnp.bfloat16),
            pltpu.VMEM(fwd_table.shape, jnp.bfloat16),
            pltpu.VMEM((HALVES, groups, ROWS, 2 * FB // HALVES), jnp.bfloat16),
            pltpu.VMEM((3, wins, 2, HALVES, ROWS, 2 * FB // HALVES), jnp.bfloat16),
            pltpu.VMEM((len(PAIRS) * ROWS, 2 * FB), jnp.float32),
            pltpu.VMEM((wins, len(TILES), ROWS, 128), SEND),
            pltpu.VMEM((groups, 3, ROWS, 128), SEND),
            pltpu.SemaphoreType.DMA((1 + QUARTERS,)),
            pltpu.SemaphoreType.DMA((HALVES, wins, 2)),
            pltpu.SemaphoreType.DMA((HALVES, wins, 2)),
            pltpu.SemaphoreType.DMA((2, wins)),
            pltpu.SemaphoreType.DMA((2, wins)),
            pltpu.SemaphoreType.DMA((4, wins)),
            pltpu.SemaphoreType.DMA((2,)),
        ],
        compiler_params=pltpu.CompilerParams(
            collective_id=0, has_side_effects=True
        ),
        name="correlate",
    )(windows, fwd_table, jnp.asarray(lag_turns()), pair_offset, pair_count.reshape(1, 1), pair_mask)
    return out.reshape(LAGS // wins, 4, CH)


def solution(mesh):
    chips, wins = mesh.shape["pair"] // 2, mesh.shape["win"]
    placed = (P("win", None, "pair"), P("pair", None), P("pair"), P("pair", None))
    return jax.shard_map(
        functools.partial(local, chips, wins),
        mesh=mesh,
        in_specs=placed,
        out_specs=P("win", "pair", None),
        check_vma=False,
    )
```

time: 249 us -> 45.4 us (0.18); the launches traced: 245 us -> 45.2 us
  waiting for transfers between devices: 146 us -> 0 us
  Pallas kernels: 0 us -> 43 us
  other arithmetic: 42.3 us -> 0 us
  matrix products: 13.8 us -> 0 us
  between operations: 13.5 us -> 0.66 us
  starting transfers between devices: 12.7 us -> 0 us
  loops' own time: 7.56 us -> 0 us
  local copies, waits for them, and re-layouts: 8.43 us -> 1.57 us
    reduce_scatter x1 -> x0, waiting for transfers between devices: 140 us -> none  [local(): lax.psum_scatter(jnp.einsum('lk,skc->lsc', inverse_rows(lag_share * lax.a...]
    pallas_call x0 -> x1, Pallas kernels: none -> 43 us  [local(): pl.pallas_call(functools.partial(kernel, chips, wins, factor), out_shape=...]
    cos x9 -> x0, other arithmetic: 39.1 us -> none  [the longest x8 33.3 us: band_table(): return jnp.concatenate([jnp.cos(phases), -jnp.sin(phases)], axis=0)]
    dot_general x17 -> x0, matrix products: 13.8 us -> none  [the longest x1 6.72 us: local(): jnp.einsum('lk,skc->lsc', inverse_rows(lag_share * lax.axis_size('win'),...]
    ppermute x4 -> x0, starting transfers between devices: 12.7 us -> none  [shifted(): return lax.ppermute(block, axis, route)]
    another operation x3 -> x0, loops' own time: 7.56 us -> none  [the longest x2 4.86 us: spectrum(): return lax.map(one_part, jnp.arange(band_parts, dtype=jnp.int32))]
    ppermute x4 -> x0, waiting for transfers between devices: 6.49 us -> none  [shifted(): return lax.ppermute(block, axis, route)]
    dynamic_slice x9 -> x0, local copies, waits for them, and re-layouts: 5.14 us -> none  [the longest x8 4.55 us: spectrum(): return lax.map(one_part, jnp.arange(band_parts, dtype=jnp.int32))]
  transfers between devices with their start and end apart: 5 -> 0, of which waited for: 4 -> 0; matrix products, arithmetic and copies ran while one was open for 12% -> 0% of each run, Pallas kernels for 0% -> 0%
where the time goes in v1:
time: 45.4 us; the launch traced here: 45.2 us
  Pallas kernels  43 us (95%)
  local copies, waits for them, and re-layouts  1.57 us (3%)
  between operations  0.66 us (1%)
    pallas_call x1, Pallas kernels, local(): pl.pallas_call(functools.partial(kernel, chips, wins, factor), out_shape=...  43 us
    unnamed x1, local copies, waits for them, and re-layouts  1.57 us

profile of v1, /device:TPU:1, one launch (start us, length us, event | category | flops | bytes accessed | tf_op | source)
XLA Modules:
  0.0 45.2 jit_solution(15739864465114984127)
XLA Ops:
  0.7 43.0 %correlate.1 = f32[256,128]{1,0:T(8,128)} custom-call(bf16[1,2048,128]{2,1,0:T(8,128)(2,1)} %x_hbm.1, bf16[4,256,1024]{2,1,0:T(8,128)(2,1)} %constant.4.clone.fwd_hbm, f32[2,512]{1,0:T(2,128)} %constant.5.clone.turn_ref, s32[1,4]{1,0:T(1,128)} %off_ref.1, s32[1,1]{1,0:T(1,128)} %bitcast.2.cnt_ref, s32[4,128]{1,0:T(4,128)} %mask_ref.1), custom_call_target="tpu_custom_call" | custom-call | tf_op jit(solution)/shard_map/correlate/pallas_call | solution.py:327
  43.6 1.6 %copy.9 = f32[64,4,128]{2,1,0:T(4,128)} copy(f32[64,4,128]{2,1,0:T(4,128)} %bitcast.3) | data formatting | bytes 262144

commit v2 on v1

v2 whole, which is shorter than its diff:
```python
import functools
import math

import jax
import jax.numpy as jnp
import numpy as np
from jax import lax
from jax.experimental import pallas as pl
from jax.experimental.pallas import tpu as pltpu
from jax.sharding import PartitionSpec as P

FB = 512
F0 = 64
LAGS = 512
LENGTH = 2048
CH = 128
SPLIT = 4
FOLD = LENGTH // SPLIT
QUARTERS = 4
HALVES = 2
ROWS = 8
SEND = jnp.bfloat16
MESH = pl.DeviceIdType.MESH
ROW = 8
OWN_PAIRS = ((2, 3), (2, 4), (2, 5), (3, 4), (3, 5))
BEFORE_PAIRS = ((0, 4), (1, 4), (1, 5))
BEYOND_PAIRS = ((2, 6), (3, 6), (3, 7))
COUNT = 12
TILES = ((0, 1), (2, 2), (3, 4), (5, 5), (6, 7), (8, 8), (9, 10))


def quarter_bins(quarter):
    steps = 8 * np.arange(FB // 8)
    return np.concatenate([steps + 2 * quarter, steps + 2 * quarter + 1])


def two_parts(table):
    high = table.astype(jnp.bfloat16)
    rest = (table - high.astype(np.float64)).astype(jnp.bfloat16)
    return high, rest


def forward_table():
    nfft = 2 * LENGTH
    parts = []
    for quarter in range(QUARTERS):
        phase = 2 * np.pi * ((F0 + quarter_bins(quarter))[:, None] * np.arange(FOLD)[None, :] % nfft) / nfft
        table = np.concatenate([np.cos(phase), -np.sin(phase)], axis=0)
        parts.append(np.concatenate(two_parts(table), axis=1))
    return np.stack(parts)


def lag_turns():
    bins = np.concatenate([quarter_bins(quarter) for quarter in range(QUARTERS)])
    phase = 2 * np.pi * ((F0 + bins) * (LAGS // 2) % (2 * LENGTH)) / (2 * LENGTH)
    return np.stack([np.cos(phase), np.sin(phase)]).astype(np.float32)


def weighted(terms):
    total = None
    for weight, value in terms:
        if abs(weight) < 1e-9:
            continue
        if abs(abs(weight) - 1.0) > 1e-9:
            value = value * np.float32(abs(weight))
        if total is None:
            total = value if weight > 0 else -value
        else:
            total = total + value if weight > 0 else total - value
    return total


def kernel(
    chips, wins, factor, x_hbm, fwd_hbm, turn_ref, off_ref, cnt_ref, mask_ref, out_ref,
    xbuf, fwd, spec, gath, acc, res, fin,
    load_sem, a_send, a_recv, z_send, z_recv, f_send, f_recv, ready,
):
    pair, win = lax.axis_index("pair"), lax.axis_index("win")
    chip, core = pair // 2, pair % 2
    place = chip % ROW
    low = place == 0
    high = (place == ROW - 1) | (chip == chips - 1)
    has_before, has_after = chip > 0, chip < chips - 1
    group = win * 2 + core
    groups = 2 * wins
    tiles = len(TILES)

    def device(chip_shift, side, there):
        return (2 * (chip + chip_shift) + side, there)

    x_copy = pltpu.make_async_copy(x_hbm.at[0], xbuf, load_sem.at[0])
    x_copy.start()
    fwd_copies = []
    for quarter in range(QUARTERS):
        copy = pltpu.make_async_copy(fwd_hbm.at[quarter], fwd.at[quarter], load_sem.at[1 + quarter])
        copy.start()
        fwd_copies.append(copy)

    barrier = pltpu.get_barrier_semaphore()

    def greet(step, carry):
        there, side = (win + step // 2) % wins, (core + step % 2) % 2

        @pl.when(step > 0)
        def _():
            pl.semaphore_signal(barrier, inc=1, device_id=device(0, side, there), device_id_type=MESH)

        @pl.when(jnp.logical_not(high))
        def _():
            pl.semaphore_signal(barrier, inc=1, device_id=device(1, side, there), device_id_type=MESH)
        return carry

    lax.fori_loop(0, groups, greet, 0)

    @pl.when(low & has_before)
    def _():
        pl.semaphore_signal(barrier, inc=1, device_id=device(-1, core, win), device_id_type=MESH)

    acc[...] = jnp.zeros_like(acc)

    @pl.when(jnp.logical_not(has_after))
    def _():
        gath[2:4] = jnp.zeros_like(gath[2:4])

    def near(step):
        turn = (step % 2) * ((step + 1) // 2) + (1 - step % 2) * (wins - step // 2)
        return (win + turn) % wins

    def exchange(half, there, side):
        return pltpu.make_async_remote_copy(
            src_ref=spec.at[half, there * 2 + side],
            dst_ref=gath.at[1, win, core, half],
            send_sem=a_send,
            recv_sem=a_recv.at[win],
            device_id=device(0, side, there),
            device_id_type=MESH,
        )

    def settle(ref, sem):
        pltpu.make_async_copy(ref, ref, sem).wait()

    x_copy.wait()
    for half in range(HALVES):
        for part in range(QUARTERS // HALVES):
            quarter = half * (QUARTERS // HALVES) + part
            fwd_copies[quarter].wait()
            wide = jnp.concatenate([xbuf[h * FOLD:(h + 1) * FOLD, :] for h in range(SPLIT)], axis=1)
            whole = jnp.dot(fwd[quarter, :, :FOLD], wide, preferred_element_type=jnp.float32)
            whole += jnp.dot(fwd[quarter, :, FOLD:], wide, preferred_element_type=jnp.float32)
            reals, imags = [], []
            for odd in range(2):
                residue = 2 * quarter + odd
                real_terms, imag_terms = [], []
                for h in range(SPLIT):
                    turn = 2 * math.pi * ((residue * h) % 8) / 8
                    real = whole[odd * 64:odd * 64 + 64, h * CH:(h + 1) * CH]
                    imag = whole[128 + odd * 64:128 + odd * 64 + 64, h * CH:(h + 1) * CH]
                    real_terms += [(math.cos(turn), real), (math.sin(turn), imag)]
                    imag_terms += [(math.cos(turn), imag), (-math.sin(turn), real)]
                reals.append(weighted(real_terms))
                imags.append(weighted(imag_terms))
            for kind, value in enumerate((reals, imags)):
                turned = jnp.concatenate(value, axis=0).T.reshape(groups, ROWS, 128)
                lane = part * 256 + kind * 128
                spec[half, :, :, lane:lane + 128] = turned.astype(jnp.bfloat16)
        if half == 0:
            later = jnp.where(high & has_after, 1, 0)
            pl.semaphore_wait(barrier, groups - 1 + jnp.where(low, 0, groups) + later)

            @pl.when(jnp.logical_not(low))
            def _():
                pl.semaphore_signal(ready.at[0], inc=1, device_id=device(-1, core, win), device_id_type=MESH)

            @pl.when(high & has_after)
            def _():
                pl.semaphore_signal(ready.at[1], inc=1, device_id=device(1, core, win), device_id_type=MESH)

        def send(step, carry, half=half):
            exchange(half, near(step // 2), (core + step % 2) % 2).start()
            return carry

        lax.fori_loop(1, groups, send, 0)
        gath[1, win, core, half] = spec[half, group]

    def forward(there, kind):
        return pltpu.make_async_remote_copy(
            src_ref=gath.at[(1, 1, 2)[kind], there],
            dst_ref=gath.at[(0, 2, 3)[kind], there],
            send_sem=z_send.at[kind],
            recv_sem=z_recv.at[kind, there],
            device_id=device((1, -1, -1)[kind], core, win),
            device_id_type=MESH,
        )

    def multiply(there, pairs, base):
        used = sorted({block for both in pairs for block in both})
        for quarter in range(QUARTERS):
            half, lane = quarter // (QUARTERS // HALVES), quarter % (QUARTERS // HALVES) * 256
            blocks = {}
            for block in used:
                both = gath[block // 2, there, block % 2, half, :, lane:lane + 256].astype(jnp.float32)
                blocks[block] = (both[:, :128], both[:, 128:])
            for index, (own, other) in enumerate(pairs):
                (own_real, own_imag), (other_real, other_imag) = blocks[own], blocks[other]
                rows = slice((base + index) * ROWS, (base + index + 1) * ROWS)
                left = slice(quarter * 256, quarter * 256 + 128)
                right = slice(quarter * 256 + 128, quarter * 256 + 256)
                acc[rows, left] += own_real * other_real + own_imag * other_imag
                acc[rows, right] += own_imag * other_real - own_real * other_imag

    lag = 3

    def travel(step, carry):
        @pl.when(step < wins)
        def _():
            there = near(step)

            @pl.when(step == 0)
            def _():
                settle(gath.at[1, win, 1 - core], a_recv.at[win])

            @pl.when(step > 0)
            def _():
                settle(gath.at[1, there], a_recv.at[there])

            @pl.when(jnp.logical_not(high))
            def _():
                @pl.when(step == 0)
                def _():
                    pl.semaphore_wait(ready.at[0], 1)

                forward(there, 0).start()

            @pl.when(has_before)
            def _():
                @pl.when(low & (step == 0))
                def _():
                    pl.semaphore_wait(ready.at[1], 1)

                forward(there, 1).start()

        @pl.when(step >= lag)
        def _():
            there = near(step - lag)

            @pl.when(has_after)
            def _():
                forward(there, 1).wait_recv()

            @pl.when(low & has_before)
            def _():
                forward(there, 2).start()

            multiply(there, OWN_PAIRS, 0)

            @pl.when(jnp.logical_not(low))
            def _():
                forward(there, 0).wait_recv()
                multiply(there, BEFORE_PAIRS, len(OWN_PAIRS))

            @pl.when(high & has_after)
            def _():
                forward(there, 2).wait_recv()
                multiply(there, BEYOND_PAIRS, len(OWN_PAIRS) + len(BEFORE_PAIRS))
        return carry

    lax.fori_loop(0, wins + lag, travel, 0)

    count = COUNT * ROWS
    stacks = jnp.zeros((count, LAGS), jnp.float32)
    for quarter in range(QUARTERS):
        bins = slice(quarter * 128, quarter * 128 + 128)
        cosine, sine = turn_ref[0:1, bins] * factor, turn_ref[1:2, bins] * factor
        real = acc[:, quarter * 256:quarter * 256 + 128]
        imag = acc[:, quarter * 256 + 128:quarter * 256 + 256]
        cross = jnp.concatenate([real * cosine + imag * sine, imag * cosine - real * sine], axis=1)
        high_part = cross.astype(jnp.bfloat16)
        rest = (cross - high_part.astype(jnp.float32)).astype(jnp.bfloat16)
        both = jnp.concatenate([high_part, rest], axis=0)
        upper = jnp.dot(both, fwd[quarter, :, :FOLD], preferred_element_type=jnp.float32)
        stacks += upper[:count] + upper[count:]
        stacks += jnp.dot(high_part, fwd[quarter, :, FOLD:], preferred_element_type=jnp.float32)
    lanes = lax.broadcasted_iota(jnp.int32, (ROWS, 128), 1)
    for column in range(LAGS // 128):
        for tile, (left, right) in enumerate(TILES):
            a = stacks[left * ROWS:(left + 1) * ROWS, column * 128:(column + 1) * 128]
            b = stacks[right * ROWS:(right + 1) * ROWS, column * 128:(column + 1) * 128]
            even = jnp.where(lanes < 64, a, pltpu.roll(b, 64, 1))
            odd = jnp.where(lanes < 64, pltpu.roll(a, 64, 1), b)
            res[2 * column * tiles + tile] = even.astype(SEND)
            res[(2 * column + 1) * tiles + tile] = odd.astype(SEND)

    def deliver(there, kind):
        first, size, slot = ((0, 2, 0), (2, 1, 0), (3, 1, 2), (4, 1, 2), (5, 1, 2), (6, 1, 2))[kind]
        return pltpu.make_async_remote_copy(
            src_ref=res.at[pl.ds(there * tiles + first, size)],
            dst_ref=fin.at[group, slot:slot + size],
            send_sem=f_send.at[kind // 2],
            recv_sem=f_recv.at[0 if kind < 2 else 1],
            device_id=device(-1 if kind // 2 == 1 else 0, kind % 2, there),
            device_id_type=MESH,
        )

    def hand_out(step, carry):
        there = near(step)

        @pl.when(jnp.logical_not(low))
        def _():
            deliver(there, 2).start()
            deliver(there, 3).start()

        for side in range(2):
            @pl.when((step > 0) | (core != side))
            def _():
                deliver(there, side).start()

                @pl.when(high)
                def _():
                    deliver(there, 4 + side).start()
        return carry

    lax.fori_loop(0, wins, hand_out, 0)
    mine = win * tiles

    @pl.when(core == 0)
    def _():
        fin[group, 0:2] = res[pl.ds(mine, 2)]

    @pl.when(core == 1)
    def _():
        fin[group, 0:1] = res[pl.ds(mine + 2, 1)]

    @pl.when(high)
    def _():
        fin[group, 2:3] = res[pl.ds(mine + 5 + core, 1)]

    settle(spec.at[:, 0:groups - 1], a_send)

    @pl.when(jnp.logical_not(high))
    def _():
        settle(gath.at[1], z_send.at[0])

    @pl.when(has_before)
    def _():
        settle(gath.at[1], z_send.at[1])

    @pl.when(low & has_before)
    def _():
        settle(gath.at[1], z_send.at[2])

    @pl.when(core == 0)
    def _():
        settle(fin.at[0:groups - 1, 0:2], f_recv.at[0])

    @pl.when(core == 1)
    def _():
        settle(fin.at[0:groups - 1, 0:1], f_recv.at[0])

    @pl.when(high)
    def _():
        settle(fin.at[0:groups - 1, 2:3], f_recv.at[1])

    @pl.when(jnp.logical_not(high))
    def _():
        settle(fin.at[:, 2:3], f_recv.at[1])

    first = fin[:, 0].astype(jnp.float32).reshape(CH, 128)
    third = fin[:, 1].astype(jnp.float32).reshape(CH, 128)
    last = fin[:, 2].astype(jnp.float32).reshape(CH, 128)
    wide_lanes = lax.broadcasted_iota(jnp.int32, (CH, 128), 1)
    second = jnp.where((wide_lanes < 64) & (core == 0), third, last)
    first, second = first.T, second.T
    choices = (first[:64], first[64:], second[:64], second[64:])
    for slot in range(4):
        offset = off_ref[0, slot]
        picked = choices[3]
        for index in range(3):
            picked = jnp.where(offset == index + 1, choices[index], picked)
        weight = mask_ref[slot:slot + 1, :].astype(jnp.float32)
        picked = jnp.where(slot < cnt_ref[0, 0], picked * weight, 0.0)
        out_ref[pl.ds(slot, 64, stride=4), :] = picked

    @pl.when(core == 0)
    def _():
        settle(res.at[0:3 * wins - 2], f_send.at[0])

    @pl.when(core == 1)
    def _():
        settle(res.at[0:3 * wins - 1], f_send.at[0])

    @pl.when(jnp.logical_not(low))
    def _():
        settle(res.at[0:groups], f_send.at[1])

    @pl.when(high)
    def _():
        settle(res.at[0:groups - 1], f_send.at[2])


def local(chips, wins, windows, pair_offset, pair_count, pair_mask):
    groups = 2 * wins
    fwd_table = jnp.asarray(forward_table())
    factor = 1.0 / (LENGTH * math.sqrt(FB * windows.shape[0] * wins))
    hbm = pl.BlockSpec(memory_space=pltpu.HBM)
    smem = pl.BlockSpec(memory_space=pltpu.SMEM)
    vmem = pl.BlockSpec(memory_space=pltpu.VMEM)
    out = pl.pallas_call(
        functools.partial(kernel, chips, wins, factor),
        out_shape=jax.ShapeDtypeStruct((LAGS // wins * 4, CH), jnp.float32),
        in_specs=[hbm, hbm, vmem, smem, smem, vmem],
        out_specs=vmem,
        scratch_shapes=[
            pltpu.VMEM((LENGTH, CH), jnp.bfloat16),
            pltpu.VMEM(fwd_table.shape, jnp.bfloat16),
            pltpu.VMEM((HALVES, groups, ROWS, 2 * FB // HALVES), jnp.bfloat16),
            pltpu.VMEM((4, wins, 2, HALVES, ROWS, 2 * FB // HALVES), jnp.bfloat16),
            pltpu.VMEM((COUNT * ROWS, 2 * FB), jnp.float32),
            pltpu.VMEM((wins * len(TILES), ROWS, 128), SEND),
            pltpu.VMEM((groups, 3, ROWS, 128), SEND),
            pltpu.SemaphoreType.DMA((1 + QUARTERS,)),
            pltpu.SemaphoreType.DMA,
            pltpu.SemaphoreType.DMA((wins,)),
            pltpu.SemaphoreType.DMA((3,)),
            pltpu.SemaphoreType.DMA((3, wins)),
            pltpu.SemaphoreType.DMA((3,)),
            pltpu.SemaphoreType.DMA((2,)),
            pltpu.SemaphoreType.REGULAR((2,)),
        ],
        compiler_params=pltpu.CompilerParams(
            collective_id=0, has_side_effects=True
        ),
        name="correlate",
    )(windows, fwd_table, jnp.asarray(lag_turns()), pair_offset, pair_count.reshape(1, 1), pair_mask)
    return out.reshape(LAGS // wins, 4, CH)


def solution(mesh):
    chips, wins = mesh.shape["pair"] // 2, mesh.shape["win"]
    placed = (P("win", None, "pair"), P("pair", None), P("pair"), P("pair", None))
    return jax.shard_map(
        functools.partial(local, chips, wins),
        mesh=mesh,
        in_specs=placed,
        out_specs=P("win", "pair", None),
        check_vma=False,
    )
```

time: 45.4 us -> 35.9 us (0.79)
  Pallas kernels: 43 us -> 33.1 us
    pallas_call x1, Pallas kernels: 43 us -> 33.1 us  [local(): pl.pallas_call(functools.partial(kernel, chips, wins, factor), out_shape=...]
where the time goes in v2:
time: 35.9 us; the launch traced here: 35.3 us
  Pallas kernels  33.1 us (92%)
  local copies, waits for them, and re-layouts  1.57 us (4%)
  between operations  0.66 us (2%)
    pallas_call x1, Pallas kernels, local(): pl.pallas_call(functools.partial(kernel, chips, wins, factor), out_shape=...  33.1 us
    unnamed x1, local copies, waits for them, and re-layouts  1.57 us

profile of v2, /device:TPU:1, one launch (start us, length us, event | category | flops | bytes accessed | tf_op | source)
XLA Modules:
  0.0 35.3 jit_solution(13115260541318292029)
XLA Ops:
  0.7 33.1 %correlate.1 = f32[256,128]{1,0:T(8,128)} custom-call(bf16[1,2048,128]{2,1,0:T(8,128)(2,1)} %x_hbm.1, bf16[4,256,1024]{2,1,0:T(8,128)(2,1)} %constant.4.clone.fwd_hbm, f32[2,512]{1,0:T(2,128)} %constant.5.clone.turn_ref, s32[1,4]{1,0:T(1,128)} %off_ref.1, s32[1,1]{1,0:T(1,128)} %bitcast.2.cnt_ref, s32[4,128]{1,0:T(4,128)} %mask_ref.1), custom_call_target="tpu_custom_call" | custom-call | tf_op jit(solution)/shard_map/correlate/pallas_call | solution.py:407
  33.7 1.6 %copy.9 = f32[64,4,128]{2,1,0:T(4,128)} copy(f32[64,4,128]{2,1,0:T(4,128)} %bitcast.3) | data formatting | bytes 262144

commit v3 on v2

--- a/solution.py
+++ b/solution.py
@@ -17,7 +17,7 @@
 SPLIT = 4
 FOLD = LENGTH // SPLIT
 QUARTERS = 4
-HALVES = 2
+HALVES = 1
 ROWS = 8
 SEND = jnp.bfloat16
 MESH = pl.DeviceIdType.MESH
@@ -71,8 +71,8 @@
 
 
 def kernel(
-    chips, wins, factor, x_hbm, fwd_hbm, turn_ref, off_ref, cnt_ref, mask_ref, out_ref,
-    xbuf, fwd, spec, gath, acc, res, fin,
+    chips, wins, factor, x_hbm, fwd_hbm, turn_hbm, off_hbm, mask_hbm, cnt_ref, out_ref,
+    xbuf, fwd, turn_ref, off_ref, mask_ref, spec, gath, acc, res, fin,
     load_sem, a_send, a_recv, z_send, z_recv, f_send, f_recv, ready,
 ):
     pair, win = lax.axis_index("pair"), lax.axis_index("win")
@@ -95,6 +95,11 @@
         copy = pltpu.make_async_copy(fwd_hbm.at[quarter], fwd.at[quarter], load_sem.at[1 + quarter])
         copy.start()
         fwd_copies.append(copy)
+    small_copies = []
+    for source, target in ((turn_hbm, turn_ref), (off_hbm, off_ref), (mask_hbm, mask_ref)):
+        copy = pltpu.make_async_copy(source, target, load_sem.at[1 + QUARTERS + len(small_copies)])
+        copy.start()
+        small_copies.append(copy)
 
     barrier = pltpu.get_barrier_semaphore()
 
@@ -208,7 +213,7 @@
                 acc[rows, left] += own_real * other_real + own_imag * other_imag
                 acc[rows, right] += own_imag * other_real - own_real * other_imag
 
-    lag = 3
+    lag = 6
 
     def travel(step, carry):
         @pl.when(step < wins)
@@ -266,6 +271,8 @@
 
     lax.fori_loop(0, wins + lag, travel, 0)
 
+    for copy in small_copies:
+        copy.wait()
     count = COUNT * ROWS
     stacks = jnp.zeros((count, LAGS), jnp.float32)
     for quarter in range(QUARTERS):
@@ -302,7 +309,7 @@
         )
 
     def hand_out(step, carry):
-        there = near(step)
+        there = near(wins - 1 - step)
 
         @pl.when(jnp.logical_not(low))
         def _():
@@ -310,7 +317,7 @@
             deliver(there, 3).start()
 
         for side in range(2):
-            @pl.when((step > 0) | (core != side))
+            @pl.when((step < wins - 1) | (core != side))
             def _():
                 deliver(there, side).start()
 
@@ -402,22 +409,25 @@
     fwd_table = jnp.asarray(forward_table())
     factor = 1.0 / (LENGTH * math.sqrt(FB * windows.shape[0] * wins))
     hbm = pl.BlockSpec(memory_space=pltpu.HBM)
-    smem = pl.BlockSpec(memory_space=pltpu.SMEM)
+    operands = (windows, fwd_table, jnp.asarray(lag_turns()), pair_offset, pair_mask)
     vmem = pl.BlockSpec(memory_space=pltpu.VMEM)
     out = pl.pallas_call(
         functools.partial(kernel, chips, wins, factor),
         out_shape=jax.ShapeDtypeStruct((LAGS // wins * 4, CH), jnp.float32),
-        in_specs=[hbm, hbm, vmem, smem, smem, vmem],
+        in_specs=[hbm] * len(operands) + [pl.BlockSpec(memory_space=pltpu.SMEM)],
         out_specs=vmem,
         scratch_shapes=[
             pltpu.VMEM((LENGTH, CH), jnp.bfloat16),
             pltpu.VMEM(fwd_table.shape, jnp.bfloat16),
+            pltpu.VMEM((2, FB), jnp.float32),
+            pltpu.SMEM(pair_offset.shape, jnp.int32),
+            pltpu.VMEM(pair_mask.shape, jnp.int32),
             pltpu.VMEM((HALVES, groups, ROWS, 2 * FB // HALVES), jnp.bfloat16),
             pltpu.VMEM((4, wins, 2, HALVES, ROWS, 2 * FB // HALVES), jnp.bfloat16),
             pltpu.VMEM((COUNT * ROWS, 2 * FB), jnp.float32),
             pltpu.VMEM((wins * len(TILES), ROWS, 128), SEND),
             pltpu.VMEM((groups, 3, ROWS, 128), SEND),
-            pltpu.SemaphoreType.DMA((1 + QUARTERS,)),
+            pltpu.SemaphoreType.DMA((4 + QUARTERS,)),
             pltpu.SemaphoreType.DMA,
             pltpu.SemaphoreType.DMA((wins,)),
             pltpu.SemaphoreType.DMA((3,)),
@@ -427,10 +437,10 @@
             pltpu.SemaphoreType.REGULAR((2,)),
         ],
         compiler_params=pltpu.CompilerParams(
-            collective_id=0, has_side_effects=True
+            collective_id=0, has_side_effects=True, vmem_limit_bytes=48 * 1024 * 1024
         ),
         name="correlate",
-    )(windows, fwd_table, jnp.asarray(lag_turns()), pair_offset, pair_count.reshape(1, 1), pair_mask)
+    )(*(pltpu.with_memory_space_constraint(operand, pltpu.HBM) for operand in operands), pair_count.reshape(1, 1))
     return out.reshape(LAGS // wins, 4, CH)
 
 

time: 35.9 us -> 31.1 us (0.87)
  Pallas kernels: 33.1 us -> 29.2 us
  local copies, waits for them, and re-layouts: 1.57 us -> 0.66 us
    pallas_call x1, Pallas kernels: 33.1 us -> 29.2 us  [local(): pl.pallas_call(functools.partial(kernel, chips, wins, factor), out_shape=...]
    unnamed x1, local copies, waits for them, and re-layouts: 1.57 us -> 0.66 us
where the time goes in v3:
time: 31.1 us; the launch traced here: 30.6 us
  Pallas kernels  29.2 us (94%)
  local copies, waits for them, and re-layouts  0.66 us (2%)
  between operations  0.66 us (2%)
    pallas_call x1, Pallas kernels, local(): pl.pallas_call(functools.partial(kernel, chips, wins, factor), out_shape=...  29.2 us
    unnamed x1, local copies, waits for them, and re-layouts  0.66 us

profile of v3, /device:TPU:1, one launch (start us, length us, event | category | flops | bytes accessed | tf_op | source)
XLA Modules:
  0.0 30.6 jit_solution(157982487130136990)
XLA Ops:
  0.7 29.2 %correlate.1 = f32[256,128]{1,0:T(8,128)S(1)} custom-call(bf16[1,2048,128]{2,1,0:T(8,128)(2,1)} %x_hbm.1, bf16[4,256,1024]{2,1,0:T(8,128)(2,1)} %constant.4.clone.fwd_hbm, f32[2,512]{1,0:T(2,128)} %constant.5.clone.turn_hbm, s32[1,4]{1,0:T(1,128)} %off_hbm.1, s32[4,128]{1,0:T(4,128)} %mask_hbm.1, s32[1,1]{1,0:T(1,128)} %bitcast.2.cnt_ref), custom_call_target="tpu_custom_call" | custom-call | tf_op jit(solution)/shard_map/correlate/pallas_call | solution.py:414
  29.9 0.7 %copy.9 = f32[64,4,128]{2,1,0:T(4,128)} copy(f32[64,4,128]{2,1,0:T(4,128)S(1)} %bitcast.3) | data formatting | bytes 262144

commit v4 on v3

--- a/solution.py
+++ b/solution.py
@@ -46,8 +46,8 @@
     for quarter in range(QUARTERS):
         phase = 2 * np.pi * ((F0 + quarter_bins(quarter))[:, None] * np.arange(FOLD)[None, :] % nfft) / nfft
         table = np.concatenate([np.cos(phase), -np.sin(phase)], axis=0)
-        parts.append(np.concatenate(two_parts(table), axis=1))
-    return np.stack(parts)
+        parts.append(table)
+    return np.stack(two_parts(np.concatenate(parts, axis=0)))
 
 
 def lag_turns():
@@ -91,10 +91,12 @@
     x_copy = pltpu.make_async_copy(x_hbm.at[0], xbuf, load_sem.at[0])
     x_copy.start()
     fwd_copies = []
-    for quarter in range(QUARTERS):
-        copy = pltpu.make_async_copy(fwd_hbm.at[quarter], fwd.at[quarter], load_sem.at[1 + quarter])
-        copy.start()
-        fwd_copies.append(copy)
+    for part in range(2):
+        for side in range(2):
+            rows = pl.ds(side * FB, FB)
+            copy = pltpu.make_async_copy(fwd_hbm.at[part, rows], fwd.at[part, rows], load_sem.at[1 + len(fwd_copies)])
+            copy.start()
+            fwd_copies.append(copy)
     small_copies = []
     for source, target in ((turn_hbm, turn_ref), (off_hbm, off_ref), (mask_hbm, mask_ref)):
         copy = pltpu.make_async_copy(source, target, load_sem.at[1 + QUARTERS + len(small_copies)])
@@ -103,33 +105,35 @@
 
     barrier = pltpu.get_barrier_semaphore()
 
-    def greet(step, carry):
-        there, side = (win + step // 2) % wins, (core + step % 2) % 2
-
-        @pl.when(step > 0)
-        def _():
-            pl.semaphore_signal(barrier, inc=1, device_id=device(0, side, there), device_id_type=MESH)
-
-        @pl.when(jnp.logical_not(high))
-        def _():
-            pl.semaphore_signal(barrier, inc=1, device_id=device(1, side, there), device_id_type=MESH)
-        return carry
-
-    lax.fori_loop(0, groups, greet, 0)
-
-    @pl.when(low & has_before)
-    def _():
-        pl.semaphore_signal(barrier, inc=1, device_id=device(-1, core, win), device_id_type=MESH)
-
-    acc[...] = jnp.zeros_like(acc)
-
-    @pl.when(jnp.logical_not(has_after))
-    def _():
-        gath[2:4] = jnp.zeros_like(gath[2:4])
-
     def near(step):
         turn = (step % 2) * ((step + 1) // 2) + (1 - step % 2) * (wins - step // 2)
         return (win + turn) % wins
+
+    def greet(step, carry):
+        there, side = near(wins - 1 - step // 2), (core + 1 + step % 2) % 2
+        pl.semaphore_signal(barrier, inc=1, device_id=device(0, side, there), device_id_type=MESH)
+        return carry
+
+    lax.fori_loop(0, groups - 1, greet, 0)
+
+    @pl.when(jnp.logical_not(high))
+    def _():
+        def greet_after(step, carry):
+            there = near(wins - 1 - step // 2)
+            pl.semaphore_signal(barrier, inc=1, device_id=device(1, step % 2, there), device_id_type=MESH)
+            return carry
+
+        lax.fori_loop(0, groups, greet_after, 0)
+
+    @pl.when(low & has_before)
+    def _():
+        pl.semaphore_signal(barrier, inc=1, device_id=device(-1, core, win), device_id_type=MESH)
+
+    acc[...] = jnp.zeros_like(acc)
+
+    @pl.when(jnp.logical_not(has_after))
+    def _():
+        gath[2:4] = jnp.zeros_like(gath[2:4])
 
     def exchange(half, there, side):
         return pltpu.make_async_remote_copy(
@@ -145,13 +149,20 @@
         pltpu.make_async_copy(ref, ref, sem).wait()
 
     x_copy.wait()
+    wide = jnp.concatenate([xbuf[h * FOLD:(h + 1) * FOLD, :] for h in range(SPLIT)], axis=1)
+    wholes = []
+    for part in range(2):
+        for side in range(2):
+            fwd_copies[2 * part + side].wait()
+            product = jnp.dot(fwd[part, side * FB:(side + 1) * FB], wide, preferred_element_type=jnp.float32)
+            if part == 0:
+                wholes.append(product)
+            else:
+                wholes[side] += product
     for half in range(HALVES):
         for part in range(QUARTERS // HALVES):
             quarter = half * (QUARTERS // HALVES) + part
-            fwd_copies[quarter].wait()
-            wide = jnp.concatenate([xbuf[h * FOLD:(h + 1) * FOLD, :] for h in range(SPLIT)], axis=1)
-            whole = jnp.dot(fwd[quarter, :, :FOLD], wide, preferred_element_type=jnp.float32)
-            whole += jnp.dot(fwd[quarter, :, FOLD:], wide, preferred_element_type=jnp.float32)
+            whole = wholes[quarter // 2][quarter % 2 * 256:quarter % 2 * 256 + 256]
             reals, imags = [], []
             for odd in range(2):
                 residue = 2 * quarter + odd
@@ -284,9 +295,9 @@
         high_part = cross.astype(jnp.bfloat16)
         rest = (cross - high_part.astype(jnp.float32)).astype(jnp.bfloat16)
         both = jnp.concatenate([high_part, rest], axis=0)
-        upper = jnp.dot(both, fwd[quarter, :, :FOLD], preferred_element_type=jnp.float32)
+        upper = jnp.dot(both, fwd[0, quarter * 256:quarter * 256 + 256], preferred_element_type=jnp.float32)
         stacks += upper[:count] + upper[count:]
-        stacks += jnp.dot(high_part, fwd[quarter, :, FOLD:], preferred_element_type=jnp.float32)
+        stacks += jnp.dot(high_part, fwd[1, quarter * 256:quarter * 256 + 256], preferred_element_type=jnp.float32)
     lanes = lax.broadcasted_iota(jnp.int32, (ROWS, 128), 1)
     for column in range(LAGS // 128):
         for tile, (left, right) in enumerate(TILES):
@@ -363,6 +374,9 @@
     def _():
         settle(fin.at[0:groups - 1, 0:1], f_recv.at[0])
 
+    first = fin[:, 0].astype(jnp.float32).reshape(CH, 128).T
+    third = fin[:, 1].astype(jnp.float32).reshape(CH, 128)
+
     @pl.when(high)
     def _():
         settle(fin.at[0:groups - 1, 2:3], f_recv.at[1])
@@ -371,12 +385,10 @@
     def _():
         settle(fin.at[:, 2:3], f_recv.at[1])
 
-    first = fin[:, 0].astype(jnp.float32).reshape(CH, 128)
-    third = fin[:, 1].astype(jnp.float32).reshape(CH, 128)
     last = fin[:, 2].astype(jnp.float32).reshape(CH, 128)
     wide_lanes = lax.broadcasted_iota(jnp.int32, (CH, 128), 1)
     second = jnp.where((wide_lanes < 64) & (core == 0), third, last)
-    first, second = first.T, second.T
+    second = second.T
     choices = (first[:64], first[64:], second[:64], second[64:])
     for slot in range(4):
         offset = off_ref[0, slot]

time: 31.1 us -> 30.8 us (level)
    pallas_call x1, Pallas kernels: 29.2 us -> 28.9 us  [local(): pl.pallas_call(functools.partial(kernel, chips, wins, factor), out_shape=...]
where the time goes in v4:
time: 30.8 us; the launch traced here: 30.2 us
  Pallas kernels  28.9 us (94%)
  local copies, waits for them, and re-layouts  0.66 us (2%)
  between operations  0.66 us (2%)
    pallas_call x1, Pallas kernels, local(): pl.pallas_call(functools.partial(kernel, chips, wins, factor), out_shape=...  28.9 us
    unnamed x1, local copies, waits for them, and re-layouts  0.66 us

profile of v4, /device:TPU:1, one launch (start us, length us, event | category | flops | bytes accessed | tf_op | source)
XLA Modules:
  0.0 30.2 jit_solution(15884822971273742637)
XLA Ops:
  0.7 28.9 %correlate.1 = f32[256,128]{1,0:T(8,128)S(1)} custom-call(bf16[1,2048,128]{2,1,0:T(8,128)(2,1)} %x_hbm.1, bf16[2,1024,512]{2,1,0:T(8,128)(2,1)} %constant.4.clone.fwd_hbm, f32[2,512]{1,0:T(2,128)} %constant.5.clone.turn_hbm, s32[1,4]{1,0:T(1,128)} %off_hbm.1, s32[4,128]{1,0:T(4,128)} %mask_hbm.1, s32[1,1]{1,0:T(1,128)} %bitcast.2.cnt_ref), custom_call_target="tpu_custom_call" | custom-call | tf_op jit(solution)/shard_map/correlate/pallas_call | solution.py:426
  29.6 0.7 %copy.9 = f32[64,4,128]{2,1,0:T(4,128)} copy(f32[64,4,128]{2,1,0:T(4,128)S(1)} %bitcast.3) | data formatting | bytes 262144
